TPU v7x, 256 devices: a whole 4x4x8 slice. The times are simulated.
256 devices in a mesh: row: 8 (over z_hi, x), col: 32 (over z_lo, y, core).
Axes of the slice: x: 4, y: 4, z: 8 (z_hi: 2, z_lo: 4; z = z_hi * 4 + z_lo), core: 2. Of those that a mesh axis runs over, the one named last changes fastest.
Arguments:
- object_field: float32 [2, 2048, 8192], P(None, 'row', 'col'), may hold values from -6 to 6
- probe: float32 [2, 4, 128, 128], replicated, may hold values from -6 to 6
- patterns: bfloat16 [8, 32, 8, 128, 128], P('row', 'col'), may hold values from 0.5 to 2
- row_scales: float32 [8, 32, 8, 128], P('row', 'col'), may hold values from 0.3 to 3
- positions: int32 [8, 32, 8, 2], P('row', 'col'), may hold values from 0 to 255
- counts: int32 [8, 32], P('row', 'col'), may hold values from 4 to 8, as said below
Outputs:
- object_out: float32 [2, 2048, 8192], P(None, 'row', 'col')
- probe_out: float32 [2, 4, 128, 128], replicated
Inputs may be any that keep to these rules, and one draw needn't show every extreme that they name: positions p >= counts[a,b] of tile (a,b) are ignored; some tile has all 8 positions live.
All inputs are finite; a program needn't handle non-finite values.
Results may differ from a plain program's by a relative error of at most 0.0003.
Values sent between devices are 32-bit elements; how exact they have to be, the bound alone decides.
No kernel may reach another device: no remote copies, remote signals or barrier semaphores. Data moves between devices by JAX's collectives and lax.ppermute only.
A program may use at most 128 MiB of HBM per device.

v0:
```python
import math
import jax
import jax.numpy as jnp
from jax import lax
from jax.sharding import PartitionSpec as P

PASSES = 2


def padded_2(block, sides, width):
    for axis, dim in sides:
        count = lax.axis_size(axis)
        forward = [(i, i + 1) for i in range(count - 1)]
        backward = [(target, source) for source, target in forward]
        low = lax.ppermute(
            lax.slice_in_dim(block, block.shape[dim] - width, None, axis=dim), axis, forward
        )
        high = lax.ppermute(lax.slice_in_dim(block, 0, width, axis=dim), axis, backward)
        block = jnp.concatenate([low, block, high], axis=dim)
    return block


def dft_tables(length):
    indices = lax.iota(jnp.int32, length)
    product = indices[:, None] * indices[None, :] % length
    angle = product.astype(jnp.float32) * (2.0 * math.pi / length)
    scaling = 1.0 / math.sqrt(length)
    cosine = jnp.cos(angle) * scaling
    sine_part = jnp.sin(angle) * scaling
    forward = jnp.concatenate(
        [jnp.concatenate([cosine, -sine_part], 1), jnp.concatenate([sine_part, cosine], 1)], 0
    )
    inverse = jnp.concatenate(
        [jnp.concatenate([cosine, sine_part], 1), jnp.concatenate([-sine_part, cosine], 1)], 0
    )
    return (forward, inverse)


def apply_table(waves, table):
    flattened = waves.reshape(-1, table.shape[0])
    result = jnp.dot(
        flattened, table, precision=lax.Precision.HIGHEST, preferred_element_type=jnp.float32
    )
    return result.reshape(waves.shape)


def transpose_pairs(waves):
    batch_size, length, pair_width = waves.shape
    return (
        waves.reshape(batch_size, length, 2, length)
        .transpose(0, 3, 2, 1)
        .reshape(batch_size, length, pair_width)
    )


def transform(waves, table):
    return transpose_pairs(apply_table(transpose_pairs(apply_table(waves, table)), table))


def fold_rim(padded, axis_number, inner, rim_width):
    middle = lax.slice_in_dim(padded, 2 * rim_width, 2 * rim_width + inner, axis=axis_number)
    lower = lax.slice_in_dim(padded, 0, rim_width, axis=axis_number)
    upper = lax.slice_in_dim(padded, inner + 3 * rim_width, inner + 4 * rim_width, axis=axis_number)
    head_part = lax.slice_in_dim(middle, 0, rim_width, axis=axis_number) + lower
    core_part = lax.slice_in_dim(middle, rim_width, inner - rim_width, axis=axis_number)
    tail_part = lax.slice_in_dim(middle, inner - rim_width, inner, axis=axis_number) + upper
    return jnp.concatenate([head_part, core_part, tail_part], axis=axis_number)


def on_device(object_field, probe, patterns, row_scales, positions, counts):
    modes = probe.shape[1]
    pattern_size = probe.shape[2]
    rim_width = pattern_size // 2
    tile_rows = object_field.shape[1]
    tile_cols = object_field.shape[2]
    position_count = positions.shape[2]
    forward, inverse = dft_tables(pattern_size)
    amplitudes = patterns[0, 0].astype(jnp.float32) * row_scales[0, 0][..., None]
    starts = positions[0, 0]
    live_flag = (lax.iota(jnp.int32, position_count) < counts[0, 0]).astype(jnp.float32)
    object_now = object_field
    probe_now = probe
    for pass_number in range(PASSES):
        extended = padded_2(object_now, (("row", 1), ("col", 2)), rim_width)
        patches = jax.vmap(
            lambda start_pair: lax.dynamic_slice(
                extended, (0, start_pair[0], start_pair[1]), (2, pattern_size, pattern_size)
            )
        )(starts)
        patch_re = patches[:, 0][:, None]
        patch_im = patches[:, 1][:, None]
        probe_re = probe_now[0][None]
        probe_im = probe_now[1][None]
        wave_re = probe_re * patch_re - probe_im * patch_im
        wave_im = probe_re * patch_im + probe_im * patch_re
        stacked = jnp.concatenate([wave_re, wave_im], axis=-1).reshape(
            -1, pattern_size, 2 * pattern_size
        )
        far_field = transform(stacked, forward).reshape(
            position_count, modes, pattern_size, 2 * pattern_size
        )
        far_re = far_field[..., :pattern_size]
        far_im = far_field[..., pattern_size:]
        intensity = jnp.sum(far_re * far_re + far_im * far_im, axis=1, keepdims=True)
        factor = amplitudes[:, None] / jnp.maximum(jnp.sqrt(intensity), 0.5)
        scaled = far_field * jnp.concatenate([factor, factor], axis=-1)
        back_wave = transform(scaled.reshape(-1, pattern_size, 2 * pattern_size), inverse)
        back_wave = back_wave.reshape(position_count, modes, pattern_size, 2 * pattern_size)
        live_mask = live_flag[:, None, None, None]
        diff_re = (back_wave[..., :pattern_size] - wave_re) * live_mask
        diff_im = (back_wave[..., pattern_size:] - wave_im) * live_mask
        contrib_re = jnp.sum(probe_re * diff_re + probe_im * diff_im, axis=1)
        contrib_im = jnp.sum(probe_re * diff_im - probe_im * diff_re, axis=1)
        updates = jnp.zeros((2, tile_rows + 2 * rim_width, tile_cols + 2 * rim_width), jnp.float32)
        for position in range(position_count):
            corner = (0, starts[position, 0], starts[position, 1])
            current = lax.dynamic_slice(updates, corner, (2, pattern_size, pattern_size))
            contribution = jnp.stack([contrib_re[position], contrib_im[position]])
            updates = lax.dynamic_update_slice(updates, current + contribution, corner)
        gradient_re = jnp.sum(patch_re * diff_re + patch_im * diff_im, axis=0)
        gradient_im = jnp.sum(patch_re * diff_im - patch_im * diff_re, axis=0)
        gradient = jnp.stack([gradient_re, gradient_im])
        weight = jnp.sum(
            live_flag[:, None, None] * (patches[:, 0] ** 2 + patches[:, 1] ** 2), axis=0
        )
        summed = padded_2(updates, (("row", 1), ("col", 2)), rim_width)
        tile_sum = fold_rim(fold_rim(summed, 1, tile_rows, rim_width), 2, tile_cols, rim_width)
        probe_peak = jnp.max(jnp.sum(probe_now[0] ** 2 + probe_now[1] ** 2, axis=0))
        object_now = object_now + tile_sum / probe_peak
        gradient_sum, weight_sum = lax.psum((gradient, weight), ("row", "col"))
        probe_now = probe_now + gradient_sum / weight_sum[None, None]
    return (object_now, probe_now)


def solution(mesh):
    placed = (
        P(None, "row", "col"),
        P(),
        P("row", "col", None, None, None),
        P("row", "col", None, None),
        P("row", "col", None, None),
        P("row", "col"),
    )
    return jax.shard_map(
        on_device,
        mesh=mesh,
        in_specs=placed,
        out_specs=(P(None, "row", "col"), P()),
        check_vma=False,
    )
```

profile of v0, /device:TPU:1, one launch (start us, length us, event | category | flops | bytes accessed | tf_op | source)
XLA Modules:
  0.0 857.3 jit_solution(2227831163460324998)
XLA Ops:
  8.2 3.9 collective-permute-start
  50.3 4.0 collective-permute-start.2
  59.1 4.4 collective-permute-done.3
  65.0 24.4 %while.2 = (s32[]{:T(128)}, f32[2,384,384]{2,1,0:T(8,128)}, s32[8,3]{0,1:T(4,128)S(1)}, f32[8,2,128,128]{3,2,0,1:T(8,128)S(1)}, s32[]{:T(128)}) while((s32[]{:T(128)}, f32[2,384,384]{2,1,0:T(8,128)}, s32[8,3]{0,1:T(4,128)S(1)}, f32[8,2,128,128]{3,2,0,1:T(8,128)S(1)}, s32[]{:T(128)}) %tuple.107), condition=%wide.while_cond, body=%wide.while_body.sunk | while | flops 2 | bytes 262261 | solution.py:86
  90.7 3.7 fusion
  94.5 7.1 fusion.47
  104.6 7.1 fusion.48
  111.7 7.3 fusion.49
  126.1 4.9 add_reduce_fusion.2
  151.4 3.6 collective-permute-start.4
  157.6 4.7 collective-permute-done.5
  168.8 3.8 collective-permute-done.6
  172.6 4.4 collective-permute-done.7
  182.4 9.1 %collective-permute-start.8 = (f32[2,64,256]{2,1,0:T(8,128)S(1)}, f32[2,64,256]{2,1,0:T(8,128)S(1)}, u32[]{:S(2)}, u32[]{:S(2)}) collective-permute-start(f32[2,64,256]{2,1,0:T(8,128)S(1)} %get-tuple-element.96), channel_id=1, source_target_pairs={{0,32},{32,64},{64,96},{96,128},{128,160},{160,192},{192,224},{1,3... | collective-permute-start | bytes 393224 | tf_op jit(solution)/shard_map/ppermute | solution.py:15
  193.5 11.1 %collective-permute-done.9 = f32[2,64,256]{2,1,0:T(8,128)S(1)} collective-permute-done((f32[2,64,256]{2,1,0:T(8,128)S(1)}, f32[2,64,256]{2,1,0:T(8,128)S(1)}, u32[]{:S(2)}, u32[]{:S(2)}) %collective-permute-start.9) | collective-permute-done | bytes 131104 | tf_op jit(solution)/shard_map/ppermute | solution.py:18
  205.6 3.6 collective-permute-start.10
  214.3 4.4 collective-permute-done.11
  221.3 28.9 %while.3 = (s32[]{:T(128)}, f32[2,384,384]{2,1,0:T(8,128)}, s32[8,3]{0,1:T(4,128)S(1)}, f32[8,2,128,128]{3,2,1,0:T(8,128)}, s32[]{:T(128)}) while((s32[]{:T(128)}, f32[2,384,384]{2,1,0:T(8,128)}, s32[8,3]{0,1:T(4,128)S(1)}, f32[8,2,128,128]{3,2,1,0:T(8,128)}, s32[]{:T(128)}) %tuple.119), condition=%wide.while_cond.1, body=%wide.while_body.1.sunk | while | flops 2 | bytes 263785 | solution.py:86
  225.5 3.0 bitcast_dynamic-update-slice_fusion.5
  232.7 3.0 bitcast_dynamic-update-slice_fusion.5
  236.3 3.0 bitcast_dynamic-update-slice_fusion.5
  243.6 3.0 bitcast_dynamic-update-slice_fusion.5
  247.2 3.0 bitcast_dynamic-update-slice_fusion.5
  255.2 265.5 %all-reduce.7.cloned.1.call-done = (f32[2,4,128,128]{3,2,1,0:T(8,128)}, f32[128,128]{1,0:T(8,128)}) async-done(((f32[2,4,128,128]{3,2,1,0:T(8,128)}, f32[128,128]{1,0:T(8,128)}), (f32[2,4,128,128]{3,2,1,0:T(8,128)}, f32[128,128]{1,0:T(8,128)})) %all-reduce.7.cloned.1.call-update) | async-done | bytes 589840 | tf_op jit(solution)/shard_map/psum | solution.py:130
  522.6 3.7 fusion.3
  526.3 7.1 fusion.50
  536.0 7.1 fusion.51
  543.1 7.4 fusion.52
  557.6 4.8 add_reduce_fusion
  588.9 5.1 collective-permute-done.13
  595.1 5.1 collective-permute-start.14
  602.2 243.2 %all-reduce.5.cloned.1.call-done = (f32[2,4,128,128]{3,2,1,0:T(8,128)}, f32[128,128]{1,0:T(8,128)}) async-done(((f32[2,4,128,128]{3,2,1,0:T(8,128)}, f32[128,128]{1,0:T(8,128)}), (f32[2,4,128,128]{3,2,1,0:T(8,128)}, f32[128,128]{1,0:T(8,128)})) %all-reduce.5.cloned.1.call-update) | async-done | bytes 589840 | tf_op jit(solution)/shard_map/psum | solution.py:130
  (213 shorter events, 158.9 us)
Async XLA Ops:
  7.2 513.5 %all-reduce.7.cloned.1.call-start = ((), (), s32[]{:S(2)}) async-start(), calls=%async_computation.1 | async-start | bytes 1179648 | tf_op jit(solution)/shard_map/psum | solution.py:130
  8.2 40.8 %collective-permute-start = (f32[2,64,256]{2,1,0:T(8,128)S(1)}, f32[2,64,256]{2,1,0:T(8,128)S(1)}, u32[]{:S(2)}, u32[]{:S(2)}) collective-permute-start(f32[2,64,256]{2,1,0:T(8,128)S(1)} %get-tuple-element.117), channel_id=1, source_target_pairs={{0,32},{32,64},{64,96},{96,128},{128,160},{160,192},{192,224},{1,3... | collective-permute-start | bytes 393224 | tf_op jit(solution)/shard_map/ppermute | solution.py:15
  12.2 38.0 %collective-permute-start.1 = (f32[2,64,256]{2,1,0:T(8,128)S(1)}, f32[2,64,256]{2,1,0:T(8,128)S(1)}, u32[]{:S(2)}, u32[]{:S(2)}) collective-permute-start(f32[2,64,256]{2,1,0:T(8,128)S(1)} %get-tuple-element.116), channel_id=1, source_target_pairs={{32,0},{64,32},{96,64},{128,96},{160,128},{192,160},{224,192},{33,... | collective-permute-start | bytes 393224 | tf_op jit(solution)/shard_map/ppermute | solution.py:18
  37.7 18.6 %copy-start = (f32[2,4,128,128]{3,2,1,0:T(8,128)S(1)}, f32[2,4,128,128]{3,2,1,0:T(8,128)}, u32[]{:S(2)}) copy-start(f32[2,4,128,128]{3,2,1,0:T(8,128)} %param.7) | copy-start | bytes 1572868
  50.3 8.8 %collective-permute-start.2 = (f32[2,384,64]{2,1,0:T(8,128)S(1)}, f32[2,384,64]{2,1,0:T(8,128)S(1)}, u32[]{:S(2)}, u32[]{:S(2)}) collective-permute-start(f32[2,384,64]{2,1,0:T(8,128)S(1)} %get-tuple-element.76), channel_id=1, source_target_pairs={{0,1},{1,2},{2,3},{3,4},{4,5},{5,6},{6,7},{7,8},{8,9},{9,10},{10,1... | collective-permute-start | bytes 589832 | tf_op jit(solution)/shard_map/ppermute | solution.py:15
  54.4 9.1 %collective-permute-start.3 = (f32[2,384,64]{2,1,0:T(8,128)S(1)}, f32[2,384,64]{2,1,0:T(8,128)S(1)}, u32[]{:S(2)}, u32[]{:S(2)}) collective-permute-start(f32[2,384,64]{2,1,0:T(8,128)S(1)} %get-tuple-element.77), channel_id=1, source_target_pairs={{1,0},{2,1},{3,2},{4,3},{5,4},{6,5},{7,6},{8,7},{9,8},{10,9},{11,1... | collective-permute-start | bytes 589832 | tf_op jit(solution)/shard_map/ppermute | solution.py:18
  57.1 32.5 %copy-start.10 = (f32[4,128,128]{2,1,0:T(8,128)}, f32[4,128,128]{2,1,0:T(8,128)S(1)}, u32[]{:S(2)}) copy-start(f32[4,128,128]{2,1,0:T(8,128)S(1)} %get-tuple-element.114) | copy-start | bytes 786436
  65.0 24.6 %copy-start.11 = (f32[4,128,128]{2,1,0:T(8,128)S(1)}, f32[4,128,128]{2,1,0:T(8,128)}, u32[]{:S(2)}) copy-start(f32[4,128,128]{2,1,0:T(8,128)} %get-tuple-element.115) | copy-start | bytes 786436
  89.5 1.2 copy-start.4
  151.4 6.2 collective-permute-start.4
  155.0 7.3 collective-permute-start.5
  163.4 9.2 %collective-permute-start.6 = (f32[2,512,64]{2,1,0:T(8,128)}, f32[2,512,64]{2,1,0:T(8,128)S(1)}, u32[]{:S(2)}, u32[]{:S(2)}) collective-permute-start(f32[2,512,64]{2,1,0:T(8,128)} %get-tuple-element.60), channel_id=1, source_target_pairs={{0,1},{1,2},{2,3},{3,4},{4,5},{5,6},{6,7},{7,8},{8,9},{9,10},{10,1... | collective-permute-start | bytes 786440 | tf_op jit(solution)/shard_map/ppermute | solution.py:15
  166.2 10.8 %collective-permute-start.7 = (f32[2,512,64]{2,1,0:T(8,128)}, f32[2,512,64]{2,1,0:T(8,128)}, u32[]{:S(2)}, u32[]{:S(2)}) collective-permute-start(f32[2,512,64]{2,1,0:T(8,128)} %get-tuple-element.61), channel_id=1, source_target_pairs={{1,0},{2,1},{3,2},{4,3},{5,4},{6,5},{7,6},{8,7},{9,8},{10,9},{11,1... | collective-permute-start | bytes 786440 | tf_op jit(solution)/shard_map/ppermute | solution.py:18
  182.4 28.8 %copy-start.15 = (f32[4,128,128]{2,1,0:T(8,128)S(1)}, f32[4,128,128]{2,1,0:T(8,128)}, u32[]{:S(2)}) copy-start(f32[4,128,128]{2,1,0:T(8,128)} %get-tuple-element.22) | copy-start | bytes 786436
  182.4 28.8 %copy-start.16 = (f32[4,128,128]{2,1,0:T(8,128)S(1)}, f32[4,128,128]{2,1,0:T(8,128)}, u32[]{:S(2)}) copy-start(f32[4,128,128]{2,1,0:T(8,128)} %get-tuple-element.25) | copy-start | bytes 786436
  182.4 11.0 %collective-permute-start.8 = (f32[2,64,256]{2,1,0:T(8,128)S(1)}, f32[2,64,256]{2,1,0:T(8,128)S(1)}, u32[]{:S(2)}, u32[]{:S(2)}) collective-permute-start(f32[2,64,256]{2,1,0:T(8,128)S(1)} %get-tuple-element.96), channel_id=1, source_target_pairs={{0,32},{32,64},{64,96},{96,128},{128,160},{160,192},{192,224},{1,3... | collective-permute-start | bytes 393224 | tf_op jit(solution)/shard_map/ppermute | solution.py:15
  191.5 13.0 %collective-permute-start.9 = (f32[2,64,256]{2,1,0:T(8,128)S(1)}, f32[2,64,256]{2,1,0:T(8,128)S(1)}, u32[]{:S(2)}, u32[]{:S(2)}) collective-permute-start(f32[2,64,256]{2,1,0:T(8,128)S(1)} %get-tuple-element.97), channel_id=1, source_target_pairs={{32,0},{64,32},{96,64},{128,96},{160,128},{192,160},{224,192},{33,... | collective-permute-start | bytes 393224 | tf_op jit(solution)/shard_map/ppermute | solution.py:18
  205.6 8.6 %collective-permute-start.10 = (f32[2,384,64]{2,1,0:T(8,128)}, f32[2,384,64]{2,1,0:T(8,128)}, u32[]{:S(2)}, u32[]{:S(2)}) collective-permute-start(f32[2,384,64]{2,1,0:T(8,128)} %get-tuple-element.74), channel_id=1, source_target_pairs={{0,1},{1,2},{2,3},{3,4},{4,5},{5,6},{6,7},{7,8},{8,9},{9,10},{10,1... | collective-permute-start | bytes 589832 | tf_op jit(solution)/shard_map/ppermute | solution.py:15
  209.2 9.4 %collective-permute-start.11 = (f32[2,384,64]{2,1,0:T(8,128)}, f32[2,384,64]{2,1,0:T(8,128)}, u32[]{:S(2)}, u32[]{:S(2)}) collective-permute-start(f32[2,384,64]{2,1,0:T(8,128)} %get-tuple-element.75), channel_id=1, source_target_pairs={{1,0},{2,1},{3,2},{4,3},{5,4},{6,5},{7,6},{8,7},{9,8},{10,9},{11,1... | collective-permute-start | bytes 589832 | tf_op jit(solution)/shard_map/ppermute | solution.py:18
  212.0 38.2 %copy-start.6 = (f32[8,2,128,128]{3,2,0,1:T(8,128)S(1)}, f32[8,2,128,128]{3,2,0,1:T(8,128)}, u32[]{:S(2)}) copy-start(f32[8,2,128,128]{3,2,0,1:T(8,128)} %copy-done.5) | copy-start | bytes 3145732
  252.3 593.1 %all-reduce.5.cloned.1.call-start = ((), (), s32[]{:S(2)}) async-start(), calls=%async_computation | async-start | bytes 1179648 | tf_op jit(solution)/shard_map/psum | solution.py:130
  253.9 268.5 %copy-start.1 = (f32[8,128,128]{2,1,0:T(8,128)}, f32[8,128,128]{2,1,0:T(8,128)S(1)}, u32[]{:S(2)}) copy-start(f32[8,128,128]{2,1,0:T(8,128)S(1)} %slice_bitcast_fusion) | copy-start | bytes 1572868
  255.2 267.3 %copy-start.2 = (f32[8,128,128]{2,1,0:T(8,128)}, f32[8,128,128]{2,1,0:T(8,128)S(1)}, u32[]{:S(2)}) copy-start(f32[8,128,128]{2,1,0:T(8,128)S(1)} %slice_bitcast_fusion.1) | copy-start | bytes 1572868
  554.6 3.0 copy-start.13
  570.1 17.1 %copy-start.17 = (f32[4,128,128]{2,1,0:T(8,128)S(1)}, f32[4,128,128]{2,1,0:T(8,128)}, u32[]{:S(2)}) copy-start(f32[4,128,128]{2,1,0:T(8,128)} %get-tuple-element.18) | copy-start | bytes 786436
  570.1 17.1 %copy-start.18 = (f32[4,128,128]{2,1,0:T(8,128)S(1)}, f32[4,128,128]{2,1,0:T(8,128)}, u32[]{:S(2)}) copy-start(f32[4,128,128]{2,1,0:T(8,128)} %get-tuple-element.21) | copy-start | bytes 786436
  583.4 5.5 collective-permute-start.12
  585.8 8.2 collective-permute-start.13
  594.0 1.1 copy-start.8
  595.1 252.2 %collective-permute-start.14 = (f32[2,512,64]{2,1,0:T(8,128)}, f32[2,512,64]{2,1,0:T(8,128)S(1)}, u32[]{:S(2)}, u32[]{:S(2)}) collective-permute-start(f32[2,512,64]{2,1,0:T(8,128)} %get-tuple-element.56), channel_id=1, source_target_pairs={{0,1},{1,2},{2,3},{3,4},{4,5},{5,6},{6,7},{7,8},{8,9},{9,10},{10,1... | collective-permute-start | bytes 786440 | tf_op jit(solution)/shard_map/ppermute | solution.py:15
  600.3 247.1 %collective-permute-start.15 = (f32[2,512,64]{2,1,0:T(8,128)}, f32[2,512,64]{2,1,0:T(8,128)S(1)}, u32[]{:S(2)}, u32[]{:S(2)}) collective-permute-start(f32[2,512,64]{2,1,0:T(8,128)} %get-tuple-element.57), channel_id=1, source_target_pairs={{1,0},{2,1},{3,2},{4,3},{5,4},{6,5},{7,6},{8,7},{9,8},{10,9},{11,1... | collective-permute-start | bytes 786440 | tf_op jit(solution)/shard_map/ppermute | solution.py:18
  845.4 2.2 copy-start.9
  (6 other events, 5.3 us)
Sparse Core Ops, SparseCore 0:
  252.5 268.1 all-reduce.6
  588.1 257.2 all-reduce.4
where the time goes:
time: 862 us; the launch traced here: 857 us
  waiting for transfers between devices  553 us (64%)
  local copies, waits for them, and re-layouts  119 us (14%)
  matrix products  50.5 us (6%)
  starting transfers between devices  48 us (6%)
  between operations  46.7 us (5%)
  other arithmetic  39.4 us (5%)
    psum x2, waiting for transfers between devices, on_device(): gradient_sum, weight_sum = lax.psum((gradient, weight), ('row', 'col'))  509 us
    gather x48, local copies, waits for them, and re-layouts  53.1 us
    dot_general x8, matrix products, apply_table(): jnp.dot(flattened, table, precision=lax.Precision.HIGHEST, preferred_elem...  50.5 us
    dynamic_update_slice x16, local copies, waits for them, and re-layouts, on_device(): updates = lax.dynamic_update_slice(updates, current + contribution, corner)  38.4 us
    ppermute x8, starting transfers between devices, padded_2(): lax.ppermute(lax.slice_in_dim(block, block.shape[dim] - width, None, axis...  34.6 us
    ppermute x8, waiting for transfers between devices, padded_2(): lax.ppermute(lax.slice_in_dim(block, 0, width, axis=dim), axis, backward)  34.1 us
  transfers between devices with their start and end apart: 18, of which 14 were waited for; matrix products, arithmetic and copies ran while one was open for 2% of the time, Pallas kernels for 0%

commit v1 on v0

--- a/solution.py
+++ b/solution.py
@@ -127,7 +127,7 @@
         tile_sum = fold_rim(fold_rim(summed, 1, tile_rows, rim_width), 2, tile_cols, rim_width)
         probe_peak = jnp.max(jnp.sum(probe_now[0] ** 2 + probe_now[1] ** 2, axis=0))
         object_now = object_now + tile_sum / probe_peak
-        gradient_sum, weight_sum = lax.psum((gradient, weight), ("row", "col"))
+        gradient_sum, weight_sum = lax.psum(lax.psum((gradient, weight), "row"), "col")
         probe_now = probe_now + gradient_sum / weight_sum[None, None]
     return (object_now, probe_now)
 

time: 862 us -> 1110 us (1.29)
  waiting for transfers between devices: 553 us -> 794 us
    psum x2 -> x4, waiting for transfers between devices: 509 us -> 744 us  [the longest x2 536 us: on_device(): lax.psum(lax.psum((gradient, weight), 'row'), 'col')]
  transfers between devices with their start and end apart: 18 -> 20, of which waited for: 14 -> 18; matrix products, arithmetic and copies ran while one was open for 2% -> 2% of each run, Pallas kernels for 0% -> 0%
where the time goes in v1:
time: 1110 us; the launch traced here: 1100 us
  waiting for transfers between devices  794 us (72%)
  local copies, waits for them, and re-layouts  121 us (11%)
  matrix products  50.5 us (5%)
  starting transfers between devices  48.5 us (4%)
  between operations  46.1 us (4%)
  other arithmetic  42 us (4%)
    psum x2, waiting for transfers between devices, on_device(): lax.psum(lax.psum((gradient, weight), 'row'), 'col')  536 us
    psum x2, waiting for transfers between devices, on_device(): lax.psum((gradient, weight), 'row')  209 us
    gather x48, local copies, waits for them, and re-layouts  54.4 us
    dot_general x8, matrix products, apply_table(): jnp.dot(flattened, table, precision=lax.Precision.HIGHEST, preferred_elem...  50.5 us
    dynamic_update_slice x16, local copies, waits for them, and re-layouts, on_device(): updates = lax.dynamic_update_slice(updates, current + contribution, corner)  38.4 us
    ppermute x8, waiting for transfers between devices, padded_2(): lax.ppermute(lax.slice_in_dim(block, 0, width, axis=dim), axis, backward)  37.7 us
    ppermute x8, starting transfers between devices, padded_2(): lax.ppermute(lax.slice_in_dim(block, block.shape[dim] - width, None, axis...  32.5 us
  transfers between devices with their start and end apart: 20, of which 18 were waited for; matrix products, arithmetic and copies ran while one was open for 2% of the time, Pallas kernels for 0%

profile of v1, /device:TPU:1, one launch (start us, length us, event | category | flops | bytes accessed | tf_op | source)
XLA Modules:
  0.0 1102.1 jit_solution(13699451702411389352)
XLA Ops:
  8.2 3.9 collective-permute-start
  50.0 4.0 collective-permute-start.2
  58.8 4.4 collective-permute-done.3
  64.7 25.0 %while.2 = (s32[]{:T(128)}, f32[2,384,384]{2,1,0:T(8,128)}, s32[8,3]{0,1:T(4,128)S(1)}, f32[8,2,128,128]{3,2,0,1:T(8,128)S(1)}, s32[]{:T(128)}) while((s32[]{:T(128)}, f32[2,384,384]{2,1,0:T(8,128)}, s32[8,3]{0,1:T(4,128)S(1)}, f32[8,2,128,128]{3,2,0,1:T(8,128)S(1)}, s32[]{:T(128)}) %tuple.107), condition=%wide.while_cond, body=%wide.while_body.sunk | while | flops 2 | bytes 262261 | solution.py:86
  91.0 3.7 fusion
  94.7 7.1 fusion.47
  104.8 7.1 fusion.48
  111.9 7.3 fusion.49
  126.4 4.9 add_reduce_fusion.2
  151.6 3.6 collective-permute-start.4
  157.8 4.7 collective-permute-done.5
  169.1 3.8 collective-permute-done.6
  172.8 4.4 collective-permute-done.7
  182.7 9.1 collective-permute-start.8
  193.7 11.1 %collective-permute-done.9 = f32[2,64,256]{2,1,0:T(8,128)S(1)} collective-permute-done((f32[2,64,256]{2,1,0:T(8,128)S(1)}, f32[2,64,256]{2,1,0:T(8,128)S(1)}, u32[]{:S(2)}, u32[]{:S(2)}) %collective-permute-start.9) | collective-permute-done | bytes 131104 | tf_op jit(solution)/shard_map/ppermute | solution.py:18
  205.9 3.6 collective-permute-start.10
  214.5 4.4 collective-permute-done.11
  221.5 29.8 %while.3 = (s32[]{:T(128)}, f32[2,384,384]{2,1,0:T(8,128)}, s32[8,3]{0,1:T(4,128)S(1)}, f32[8,2,128,128]{3,2,1,0:T(8,128)}, s32[]{:T(128)}) while((s32[]{:T(128)}, f32[2,384,384]{2,1,0:T(8,128)}, s32[8,3]{0,1:T(4,128)S(1)}, f32[8,2,128,128]{3,2,1,0:T(8,128)}, s32[]{:T(128)}) %tuple.125), condition=%wide.while_cond.1, body=%wide.while_body.1.sunk | while | flops 2 | bytes 263785 | solution.py:86
  229.6 3.1 bitcast_dynamic-update-slice_fusion.5
  233.4 3.1 bitcast_dynamic-update-slice_fusion.5
  253.5 119.5 %all-reduce.15.cloned.1.call-done = (f32[2,4,128,128]{3,2,1,0:T(8,128)}, f32[128,128]{1,0:T(8,128)}) async-done(((f32[2,4,128,128]{3,2,1,0:T(8,128)}, f32[128,128]{1,0:T(8,128)}), (f32[2,4,128,128]{3,2,1,0:T(8,128)}, f32[128,128]{1,0:T(8,128)})) %all-reduce.15.cloned.1.call-update) | async-done | bytes 589840 | tf_op jit(solution)/shard_map/psum | solution.py:130
  375.8 268.3 %all-reduce.11.cloned.1.call-done = (f32[2,4,128,128]{3,2,1,0:T(8,128)}, f32[128,128]{1,0:T(8,128)}) async-done(((f32[2,4,128,128]{3,2,1,0:T(8,128)}, f32[128,128]{1,0:T(8,128)}), (f32[2,4,128,128]{3,2,1,0:T(8,128)}, f32[128,128]{1,0:T(8,128)})) %all-reduce.11.cloned.1.call-update) | async-done | bytes 589840 | tf_op jit(solution)/shard_map/psum | solution.py:130
  646.0 3.7 fusion.3
  649.8 7.1 fusion.50
  659.4 7.1 fusion.51
  666.5 7.4 fusion.52
  681.0 4.8 add_reduce_fusion
  712.2 4.4 collective-permute-done.13
  720.8 4.5 collective-permute-start.15
  727.2 4.3 collective-permute-done.15
  733.4 89.1 %all-reduce.13.cloned.1.call-done = (f32[2,4,128,128]{3,2,1,0:T(8,128)}, f32[128,128]{1,0:T(8,128)}) async-done(((f32[2,4,128,128]{3,2,1,0:T(8,128)}, f32[128,128]{1,0:T(8,128)}), (f32[2,4,128,128]{3,2,1,0:T(8,128)}, f32[128,128]{1,0:T(8,128)})) %all-reduce.13.cloned.1.call-update) | async-done | bytes 589840 | tf_op jit(solution)/shard_map/psum | solution.py:130
  825.9 267.6 %all-reduce.9.cloned.1.call-done = (f32[2,4,128,128]{3,2,1,0:T(8,128)}, f32[128,128]{1,0:T(8,128)}) async-done(((f32[2,4,128,128]{3,2,1,0:T(8,128)}, f32[128,128]{1,0:T(8,128)}), (f32[2,4,128,128]{3,2,1,0:T(8,128)}, f32[128,128]{1,0:T(8,128)})) %all-reduce.9.cloned.1.call-update) | async-done | bytes 589840 | tf_op jit(solution)/shard_map/psum | solution.py:130
  (219 shorter events, 174.7 us)
Async XLA Ops:
  7.2 365.8 %all-reduce.15.cloned.1.call-start = ((), (), s32[]{:S(2)}) async-start(), calls=%async_computation.3 | async-start | bytes 1179648 | tf_op jit(solution)/shard_map/psum | solution.py:130
  8.2 40.5 %collective-permute-start = (f32[2,64,256]{2,1,0:T(8,128)S(1)}, f32[2,64,256]{2,1,0:T(8,128)S(1)}, u32[]{:S(2)}, u32[]{:S(2)}) collective-permute-start(f32[2,64,256]{2,1,0:T(8,128)S(1)} %get-tuple-element.121), channel_id=1, source_target_pairs={{0,32},{32,64},{64,96},{96,128},{128,160},{160,192},{192,224},{1,3... | collective-permute-start | bytes 393224 | tf_op jit(solution)/shard_map/ppermute | solution.py:15
  12.2 37.7 %collective-permute-start.1 = (f32[2,64,256]{2,1,0:T(8,128)S(1)}, f32[2,64,256]{2,1,0:T(8,128)S(1)}, u32[]{:S(2)}, u32[]{:S(2)}) collective-permute-start(f32[2,64,256]{2,1,0:T(8,128)S(1)} %get-tuple-element.120), channel_id=1, source_target_pairs={{32,0},{64,32},{96,64},{128,96},{160,128},{192,160},{224,192},{33,... | collective-permute-start | bytes 393224 | tf_op jit(solution)/shard_map/ppermute | solution.py:18
  37.4 18.5 %copy-start = (f32[2,4,128,128]{3,2,1,0:T(8,128)S(1)}, f32[2,4,128,128]{3,2,1,0:T(8,128)}, u32[]{:S(2)}) copy-start(f32[2,4,128,128]{3,2,1,0:T(8,128)} %param.7) | copy-start | bytes 1572868
  50.0 8.8 collective-permute-start.2
  54.1 9.1 collective-permute-start.3
  56.8 33.0 %copy-start.10 = (f32[4,128,128]{2,1,0:T(8,128)}, f32[4,128,128]{2,1,0:T(8,128)S(1)}, u32[]{:S(2)}) copy-start(f32[4,128,128]{2,1,0:T(8,128)S(1)} %get-tuple-element.118) | copy-start | bytes 786436
  64.7 25.1 %copy-start.11 = (f32[4,128,128]{2,1,0:T(8,128)S(1)}, f32[4,128,128]{2,1,0:T(8,128)}, u32[]{:S(2)}) copy-start(f32[4,128,128]{2,1,0:T(8,128)} %get-tuple-element.119) | copy-start | bytes 786436
  151.6 6.2 collective-permute-start.4
  155.2 7.3 collective-permute-start.5
  163.6 9.2 collective-permute-start.6
  166.4 10.8 collective-permute-start.7
  182.6 28.8 %copy-start.15 = (f32[4,128,128]{2,1,0:T(8,128)S(1)}, f32[4,128,128]{2,1,0:T(8,128)}, u32[]{:S(2)}) copy-start(f32[4,128,128]{2,1,0:T(8,128)} %get-tuple-element.22) | copy-start | bytes 786436
  182.6 28.8 %copy-start.16 = (f32[4,128,128]{2,1,0:T(8,128)S(1)}, f32[4,128,128]{2,1,0:T(8,128)}, u32[]{:S(2)}) copy-start(f32[4,128,128]{2,1,0:T(8,128)} %get-tuple-element.25) | copy-start | bytes 786436
  182.7 11.0 %collective-permute-start.8 = (f32[2,64,256]{2,1,0:T(8,128)S(1)}, f32[2,64,256]{2,1,0:T(8,128)S(1)}, u32[]{:S(2)}, u32[]{:S(2)}) collective-permute-start(f32[2,64,256]{2,1,0:T(8,128)S(1)} %get-tuple-element.100), channel_id=1, source_target_pairs={{0,32},{32,64},{64,96},{96,128},{128,160},{160,192},{192,224},{1,3... | collective-permute-start | bytes 393224 | tf_op jit(solution)/shard_map/ppermute | solution.py:15
  191.8 13.0 %collective-permute-start.9 = (f32[2,64,256]{2,1,0:T(8,128)S(1)}, f32[2,64,256]{2,1,0:T(8,128)S(1)}, u32[]{:S(2)}, u32[]{:S(2)}) collective-permute-start(f32[2,64,256]{2,1,0:T(8,128)S(1)} %get-tuple-element.101), channel_id=1, source_target_pairs={{32,0},{64,32},{96,64},{128,96},{160,128},{192,160},{224,192},{33,... | collective-permute-start | bytes 393224 | tf_op jit(solution)/shard_map/ppermute | solution.py:18
  205.9 8.6 collective-permute-start.10
  209.5 9.4 collective-permute-start.11
  212.3 39.0 %copy-start.6 = (f32[8,2,128,128]{3,2,0,1:T(8,128)S(1)}, f32[8,2,128,128]{3,2,0,1:T(8,128)}, u32[]{:S(2)}) copy-start(f32[8,2,128,128]{3,2,0,1:T(8,128)} %copy-done.5) | copy-start | bytes 3145732
  253.4 390.7 %all-reduce.11.cloned.1.call-start = ((), (), s32[]{:S(2)}) async-start(), calls=%async_computation.1 | async-start | bytes 1179648 | tf_op jit(solution)/shard_map/psum | solution.py:130
  373.0 449.5 %all-reduce.13.cloned.1.call-start = ((), (), s32[]{:S(2)}) async-start(), calls=%async_computation.2 | async-start | bytes 1179648 | tf_op jit(solution)/shard_map/psum | solution.py:130
  374.5 271.3 %copy-start.1 = (f32[8,128,128]{2,1,0:T(8,128)}, f32[8,128,128]{2,1,0:T(8,128)S(1)}, u32[]{:S(2)}) copy-start(f32[8,128,128]{2,1,0:T(8,128)S(1)} %slice_bitcast_fusion) | copy-start | bytes 1572868
  375.8 270.1 %copy-start.2 = (f32[8,128,128]{2,1,0:T(8,128)}, f32[8,128,128]{2,1,0:T(8,128)S(1)}, u32[]{:S(2)}) copy-start(f32[8,128,128]{2,1,0:T(8,128)S(1)} %slice_bitcast_fusion.1) | copy-start | bytes 1572868
  678.1 3.0 copy-start.13
  693.5 17.1 %copy-start.17 = (f32[4,128,128]{2,1,0:T(8,128)S(1)}, f32[4,128,128]{2,1,0:T(8,128)}, u32[]{:S(2)}) copy-start(f32[4,128,128]{2,1,0:T(8,128)} %get-tuple-element.18) | copy-start | bytes 786436
  693.5 17.1 %copy-start.18 = (f32[4,128,128]{2,1,0:T(8,128)S(1)}, f32[4,128,128]{2,1,0:T(8,128)}, u32[]{:S(2)}) copy-start(f32[4,128,128]{2,1,0:T(8,128)} %get-tuple-element.21) | copy-start | bytes 786436
  706.9 5.3 collective-permute-start.12
  709.3 7.3 collective-permute-start.13
  711.5 382.0 %all-reduce.9.cloned.1.call-start = ((), (), s32[]{:S(2)}) async-start(), calls=%async_computation | async-start | bytes 1179648 | tf_op jit(solution)/shard_map/psum | solution.py:130
  717.7 9.5 collective-permute-start.14
  720.8 10.7 collective-permute-start.15
  726.0 6.4 copy-start.9
  (8 other events, 7.6 us)
Sparse Core Ops, SparseCore 0:
  253.5 119.3 all-reduce.14
  375.7 268.3 all-reduce.10
  711.6 110.8 all-reduce.12
  825.0 268.3 all-reduce.8
